TPU v7x, 32 devices: a whole 2x2x4 slice. The times are simulated.
32 devices in a mesh: row: 8 (over z, x), col: 4 (over y, core).
Axes of the slice: x: 2, y: 2, z: 4, core: 2. Of those that a mesh axis runs over, the one named last changes fastest.
Arguments:
- patches: bfloat16 [16384, 1024], P('row', 'col'), may hold values from -16 to 16
- w_query: bfloat16 [1024, 1024], P('row', 'col'), may hold values from -0.1875 to 0.1875
- w_key: bfloat16 [1024, 1024], P('row', 'col'), may hold values from -0.1875 to 0.1875
- w_value: bfloat16 [1024, 1024], P('row', 'col'), may hold values from -0.1875 to 0.1875
- w_out: bfloat16 [1024, 1024], P('col', 'row'), may hold values from -2 to 2
- w_gate: bfloat16 [1024, 2816], P('row', 'col'), may hold values from -0.1875 to 0.1875
- w_up: bfloat16 [1024, 2816], P('row', 'col'), may hold values from -0.1875 to 0.1875
- w_down: bfloat16 [2816, 1024], P('col', 'row'), may hold values from -0.109375 to 0.109375
- gain_attn: bfloat16 [1024], P('row'), may hold values from 0.5 to 1.5
- gain_mlp: bfloat16 [1024], P('row'), may hold values from 0.5 to 1.5
- lengths: int32 [16], P('row'), may hold values from 256 to 1024, as said below
- cotangent: bfloat16 [16384, 1024], P('row', 'col'), may hold values from -6 to 6
Outputs:
- output: bfloat16 [16384, 1024], P('row', 'col')
- grad_patches: float32 [16384, 1024], P('row', 'col')
- grad_query: float32 [1024, 1024], P('row', 'col')
- grad_key: float32 [1024, 1024], P('row', 'col')
- grad_value: float32 [1024, 1024], P('row', 'col')
- grad_out: float32 [1024, 1024], P('col', 'row')
- grad_gate: float32 [1024, 2816], P('row', 'col')
- grad_up: float32 [1024, 2816], P('row', 'col')
- grad_down: float32 [2816, 1024], P('col', 'row')
- grad_gain_attn: float32 [1024], P('row')
- grad_gain_mlp: float32 [1024], P('row')
Inputs may be any that keep to these rules, and one draw needn't show every extreme that they name: Each sequence's valid slots are its first lengths[s]; every draw has a sequence with all 1024 slots valid and one with 256.
All inputs are finite; a program needn't handle non-finite values.
Results may differ from a plain program's by a relative error of at most 0.012.
The roundings to bfloat16 on the way count: a program that leaves them out, or rounds other values in their place, can miss the bound.
Values may be sent and summed in bfloat16 or wider, within the bound.
No kernel may reach another device: no remote copies, remote signals or barrier semaphores. Data moves between devices by JAX's collectives and lax.ppermute only.
A program may use at most 192 MiB of HBM per device.

v0:
```python
import jax
import jax.numpy as jnp
from jax import lax
from jax.sharding import PartitionSpec as P

HEAD_DIM = 64
EPSILON = 1e-06
MASKED = -1000000000.0


def times_trans(left, right):
    return lax.dot_general(
        left, right, (((1,), (1,)), ((), ())), preferred_element_type=jnp.float32
    )


def contract_rows(left, right):
    return lax.dot_general(
        left, right, (((0,), (0,)), ((), ())), preferred_element_type=jnp.float32
    )


def shards(
    patches,
    w_query,
    w_key,
    w_value,
    w_out,
    w_gate,
    w_up,
    w_down,
    gain_attn,
    gain_mlp,
    lengths,
    cotangent,
):
    slab = patches.shape[1]
    width = slab * lax.axis_size("col")
    col_start = lax.axis_index("col") * slab
    micro = lengths.shape[0]
    seq = patches.shape[0] // micro
    heads_here = w_query.shape[1] // HEAD_DIM
    scale = HEAD_DIM ** (-0.5)
    block = min(512, seq)
    positions = lax.iota(jnp.int32, seq)

    def fetch():
        return (
            lax.all_gather(w_query, "row", axis=0, tiled=True),
            lax.all_gather(w_key, "row", axis=0, tiled=True),
            lax.all_gather(w_value, "row", axis=0, tiled=True),
            lax.all_gather(w_out, "row", axis=1, tiled=True),
            lax.all_gather(w_gate, "row", axis=0, tiled=True),
            lax.all_gather(w_up, "row", axis=0, tiled=True),
            lax.all_gather(w_down, "row", axis=1, tiled=True),
            lax.all_gather(gain_attn, "row", axis=0, tiled=True),
            lax.all_gather(gain_mlp, "row", axis=0, tiled=True),
        )

    def to_full(values_own):
        return lax.all_gather(values_own, "col", axis=1, tiled=True)

    def reduce_cols(partial_value):
        return lax.psum_scatter(partial_value, "col", scatter_dimension=1, tiled=True)

    def norm_forward(rows_own, gain_whole):
        total = lax.psum(jnp.sum(rows_own * rows_own, axis=1), "col")
        rstd = lax.rsqrt(total / width + EPSILON)
        gain_own = lax.dynamic_slice_in_dim(gain_whole, col_start, slab).astype(jnp.float32)
        normed = (rows_own * rstd[:, None] * gain_own).astype(jnp.bfloat16)
        return (normed, rstd, gain_own)

    def norm_backward(grad_partial, rows_own, rstd, gain_own):
        grad_normed = reduce_cols(grad_partial)
        weighted = grad_normed * gain_own
        gain_piece = jnp.sum(grad_normed * rows_own * rstd[:, None], axis=0)
        gain_whole = lax.dynamic_update_slice_in_dim(
            jnp.zeros((width,), jnp.float32), gain_piece, col_start, 0
        )
        stat, gain_grad = lax.psum((jnp.sum(weighted * rows_own, axis=1), gain_whole), "col")
        grad_rows = (
            rstd[:, None] * weighted - rows_own * (rstd * rstd * rstd * stat / width)[:, None]
        )
        return (grad_rows, gain_grad)

    def split_heads(tensor):
        return jnp.transpose(tensor.reshape(seq, heads_here, HEAD_DIM), (1, 0, 2))

    def join_heads(tensor):
        return jnp.transpose(tensor, (1, 0, 2)).reshape(seq, heads_here * HEAD_DIM)

    def block_scores(query_h, key_h, first_row, last_row, length):
        raw = times_trans(query_h[first_row:last_row], key_h[:last_row]) * scale
        keep = (positions[None, :last_row] <= positions[first_row:last_row, None]) & (
            positions[None, :last_row] < length
        )
        return jnp.where(keep, raw, MASKED)

    outputs = []
    input_grads = []
    totals = None
    for batch in range(micro):
        first_slot = batch * seq
        weights_now = fetch()
        (
            query_full,
            key_full,
            value_full,
            out_full,
            gate_full,
            up_full,
            down_full,
            attn_gain,
            mlp_gain,
        ) = weights_now
        rows_own = patches[first_slot : first_slot + seq].astype(jnp.float32)
        length = lengths[batch]
        valid = (positions < length)[:, None]
        normed_own, rstd_one, gain_one = norm_forward(rows_own, attn_gain)
        normed_one = to_full(normed_own)
        queries = split_heads(
            jnp.dot(normed_one, query_full, preferred_element_type=jnp.float32).astype(jnp.bfloat16)
        )
        keys_all = split_heads(
            jnp.dot(normed_one, key_full, preferred_element_type=jnp.float32).astype(jnp.bfloat16)
        )
        values_all = split_heads(
            jnp.dot(normed_one, value_full, preferred_element_type=jnp.float32).astype(jnp.bfloat16)
        )

        def attend_per_head(operands):
            query_h, key_h, value_h = operands
            pieces = []
            totals = []
            for index in range(seq // block):
                first_row = index * block
                last_row = first_row + block
                scores = block_scores(query_h, key_h, first_row, last_row, length)
                peak = jnp.max(scores, axis=1, keepdims=True)
                expo = jnp.exp(scores - peak)
                denom = jnp.sum(expo, axis=1, keepdims=True)
                probs = (expo / denom).astype(jnp.bfloat16)
                pieces.append(
                    jnp.dot(probs, value_h[:last_row], preferred_element_type=jnp.float32)
                )
                totals.append((peak + jnp.log(denom))[:, 0])
            return (jnp.concatenate(pieces, axis=0), jnp.concatenate(totals, axis=0))

        attended, logsum = lax.map(attend_per_head, (queries, keys_all, values_all))
        attended = join_heads(attended).astype(jnp.bfloat16)
        hstate = rows_own + reduce_cols(
            jnp.dot(attended, out_full, preferred_element_type=jnp.float32)
        )
        normed_own_two, rstd_two, gain_two = norm_forward(hstate, mlp_gain)
        normed_two = to_full(normed_own_two)
        gate = jnp.dot(normed_two, gate_full, preferred_element_type=jnp.float32)
        upward = jnp.dot(normed_two, up_full, preferred_element_type=jnp.float32)
        sigmoid_gate = jax.nn.sigmoid(gate)
        activated = gate * sigmoid_gate
        hidden = (activated * upward).astype(jnp.bfloat16)
        mixed = reduce_cols(jnp.dot(hidden, down_full, preferred_element_type=jnp.float32))
        outputs.append(jnp.where(valid, hstate + mixed, 0.0).astype(jnp.bfloat16))
        weights_back = fetch()
        (
            query_full,
            key_full,
            value_full,
            out_full,
            gate_full,
            up_full,
            down_full,
            attn_gain,
            mlp_gain,
        ) = weights_back
        grad_mixed = jnp.where(
            valid, cotangent[first_slot : first_slot + seq], jnp.zeros((), jnp.bfloat16)
        )
        grad_mixed_full = to_full(grad_mixed)
        grad_hidden = times_trans(grad_mixed_full, down_full)
        down_grad = contract_rows(hidden, grad_mixed_full)
        grad_gate_act = (
            grad_hidden * upward * sigmoid_gate * (1.0 + gate * (1.0 - sigmoid_gate))
        ).astype(jnp.bfloat16)
        grad_up_act = (grad_hidden * activated).astype(jnp.bfloat16)
        gate_grad = contract_rows(normed_two, grad_gate_act)
        up_grad = contract_rows(normed_two, grad_up_act)
        grad_normed_two = times_trans(grad_gate_act, gate_full) + times_trans(grad_up_act, up_full)
        grad_norm_two, mlp_gain_grad = norm_backward(grad_normed_two, hstate, rstd_two, gain_two)
        grad_hstate = grad_mixed.astype(jnp.float32) + grad_norm_two
        grad_branch = to_full(grad_hstate.astype(jnp.bfloat16))
        out_grad = contract_rows(attended, grad_branch)
        grad_attended = split_heads(times_trans(grad_branch, out_full).astype(jnp.bfloat16))

        def per_head(operands):
            query_h, key_h, value_h, grad_h, logsum_h = operands
            query_parts = []
            key_grad = jnp.zeros((seq, HEAD_DIM), jnp.float32)
            value_grad = jnp.zeros((seq, HEAD_DIM), jnp.float32)
            for index in range(seq // block):
                first_row = index * block
                last_row = first_row + block
                scores = block_scores(query_h, key_h, first_row, last_row, length)
                probs = jnp.exp(scores - logsum_h[first_row:last_row, None])
                rounded = probs.astype(jnp.bfloat16)
                grad_probs = times_trans(grad_h[first_row:last_row], value_h[:last_row])
                inner = jnp.sum(probs * grad_probs, axis=1, keepdims=True)
                grad_scores = (probs * (grad_probs - inner)).astype(jnp.bfloat16)
                query_parts.append(
                    jnp.dot(grad_scores, key_h[:last_row], preferred_element_type=jnp.float32)
                    * scale
                )
                key_grad = key_grad.at[:last_row].add(
                    contract_rows(grad_scores, query_h[first_row:last_row]) * scale
                )
                value_grad = value_grad.at[:last_row].add(
                    contract_rows(rounded, grad_h[first_row:last_row])
                )
            query_grad = jnp.concatenate(query_parts, axis=0)
            return (
                query_grad.astype(jnp.bfloat16),
                key_grad.astype(jnp.bfloat16),
                value_grad.astype(jnp.bfloat16),
            )

        grad_queries, grad_keys, grad_values = lax.map(
            per_head, (queries, keys_all, values_all, grad_attended, logsum)
        )
        grad_queries = join_heads(grad_queries)
        grad_keys = join_heads(grad_keys)
        grad_values = join_heads(grad_values)
        query_grad = contract_rows(normed_one, grad_queries)
        key_grad = contract_rows(normed_one, grad_keys)
        value_grad = contract_rows(normed_one, grad_values)
        grad_normed_one = (
            times_trans(grad_queries, query_full)
            + times_trans(grad_keys, key_full)
            + times_trans(grad_values, value_full)
        )
        grad_norm_one, attn_gain_grad = norm_backward(grad_normed_one, rows_own, rstd_one, gain_one)
        input_grads.append(grad_hstate + grad_norm_one)
        local_terms = (
            query_grad,
            key_grad,
            value_grad,
            out_grad,
            gate_grad,
            up_grad,
            down_grad,
            attn_gain_grad,
            mlp_gain_grad,
        )
        reduced = (
            lax.psum_scatter(local_terms[0], "row", scatter_dimension=0, tiled=True),
            lax.psum_scatter(local_terms[1], "row", scatter_dimension=0, tiled=True),
            lax.psum_scatter(local_terms[2], "row", scatter_dimension=0, tiled=True),
            lax.psum_scatter(local_terms[3], "row", scatter_dimension=1, tiled=True),
            lax.psum_scatter(local_terms[4], "row", scatter_dimension=0, tiled=True),
            lax.psum_scatter(local_terms[5], "row", scatter_dimension=0, tiled=True),
            lax.psum_scatter(local_terms[6], "row", scatter_dimension=1, tiled=True),
            lax.psum_scatter(local_terms[7], "row", scatter_dimension=0, tiled=True),
            lax.psum_scatter(local_terms[8], "row", scatter_dimension=0, tiled=True),
        )
        totals = reduced if totals is None else jax.tree.map(jnp.add, totals, reduced)
    return (
        jnp.concatenate(outputs, axis=0),
        jnp.concatenate(input_grads, axis=0),
        totals[0],
        totals[1],
        totals[2],
        totals[3],
        totals[4],
        totals[5],
        totals[6],
        totals[7],
        totals[8],
    )


def solution(mesh):
    placed = (
        P("row", "col"),
        P("row", "col"),
        P("row", "col"),
        P("row", "col"),
        P("col", "row"),
        P("row", "col"),
        P("row", "col"),
        P("col", "row"),
        P("row"),
        P("row"),
        P("row"),
        P("row", "col"),
    )
    return jax.shard_map(
        shards,
        mesh=mesh,
        in_specs=placed,
        out_specs=(
            P("row", "col"),
            P("row", "col"),
            P("row", "col"),
            P("row", "col"),
            P("row", "col"),
            P("col", "row"),
            P("row", "col"),
            P("row", "col"),
            P("col", "row"),
            P("row"),
            P("row"),
        ),
        check_vma=False,
    )
```

profile of v0, /device:TPU:0, one launch (start us, length us, event | category | flops | bytes accessed | tf_op | source)
XLA Modules:
  0.0 1450.2 jit_solution(8379913101905790760)
XLA Ops:
  8.1 22.3 %all-gather = bf16[8,1,128]{2,1,0:T(2,128)(2,1)S(1)} all-gather(bf16[1,1,128]{2,1,0:T(2,128)(2,1)} %bitcast.471), channel_id=1, replica_groups=mesh['row'=8,'col'=4] {'row'}, dimensions={0}, use_global_device_ids=true | all-gather | bytes 2304 | tf_op jit(solution)/shard_map/all_gather | solution.py:56
  32.1 5.7 all-reduce.10
  37.9 2.5 fusion.102
  41.3 31.7 %all_gather.36 = bf16[1024,256]{1,0:T(8,128)(2,1)S(1)} all-gather(bf16[128,256]{1,0:T(8,128)(2,1)S(1)} %copy-done.36), channel_id=1, replica_groups=mesh['row'=8,'col'=4] {'row'}, dimensions={0}, use_global_device_ids=true | all-gather | bytes 589824 | tf_op jit(solution)/shard_map/all_gather | solution.py:49
  73.0 31.4 %all_gather.37 = bf16[1024,256]{1,0:T(8,128)(2,1)S(1)} all-gather(bf16[128,256]{1,0:T(8,128)(2,1)S(1)} %copy-done.37), channel_id=1, replica_groups=mesh['row'=8,'col'=4] {'row'}, dimensions={0}, use_global_device_ids=true | all-gather | bytes 589824 | tf_op jit(solution)/shard_map/all_gather | solution.py:50
  104.5 33.4 %all_gather.38 = bf16[1024,256]{1,0:T(8,128)(2,1)} all-gather(bf16[128,256]{1,0:T(8,128)(2,1)S(1)} %copy-done.38), channel_id=1, replica_groups=mesh['row'=8,'col'=4] {'row'}, dimensions={0}, use_global_device_ids=true | all-gather | bytes 589824 | tf_op jit(solution)/shard_map/all_gather | solution.py:51
  138.5 28.1 %all_gather.39 = bf16[256,1024]{1,0:T(8,128)(2,1)} all-gather(bf16[256,128]{1,0:T(8,128)(2,1)S(1)} %copy-done.39), channel_id=1, replica_groups=mesh['row'=8,'col'=4] {'row'}, dimensions={1}, use_global_device_ids=true | all-gather | bytes 589824 | tf_op jit(solution)/shard_map/all_gather | solution.py:52
  166.6 3.3 convolution_convert_fusion.7
  179.1 34.7 %while.74 = (s32[]{:T(128)}, bf16[4,1024,64]{1,2,0:T(8,128)(2,1)}, f32[4,1024]{1,0:T(4,128)S(1)}, s32[1024]{0:T(1024)S(1)}, s32[]{:T(128)}, /*index=5*/bf16[4,10...) while((s32[]{:T(128)}, bf16[4,1024,64]{1,2,0:T(8,128)(2,1)}, ...), condition=%wide.region_7.8_spmd.clone, body=%wide.region_2.7_spmd.clone.sunk | while | flops 209454592 | bytes 10959497 | solution.py:149
  213.8 3.9 fusion.135
  218.8 3.3 convolution_convert_fusion.4
  231.3 34.8 %while.75 = (s32[]{:T(128)}, bf16[4,1024,64]{1,2,0:T(8,128)(2,1)}, f32[4,1024]{1,0:T(4,128)S(1)}, s32[1024]{0:T(1024)S(1)}, s32[]{:T(128)}, /*index=5*/bf16[4,10...) while((s32[]{:T(128)}, bf16[4,1024,64]{1,2,0:T(8,128)(2,1)}, ...), condition=%wide.region_19.20_spmd.clone, body=%wide.region_14.19_spmd.clone.sunk | while | flops 209454592 | bytes 10959497 | solution.py:149
  266.1 3.9 fusion.139
  270.7 16.3 %all-gather.1 = bf16[8,1,128]{2,1,0:T(2,128)(2,1)S(1)} all-gather(bf16[1,1,128]{2,1,0:T(2,128)(2,1)S(1)} %bitcast.472), channel_id=1, replica_groups=mesh['row'=8,'col'=4] {'row'}, dimensions={0}, use_global_device_ids=true | all-gather | bytes 2304 | tf_op jit(solution)/shard_map/all_gather | solution.py:57
  287.1 25.6 %reduce-scatter.20.cloned.1.call-done = f32[1024,256]{1,0:T(8,128)} async-done(((f32[1024,1024]{1,0:T(8,128)}), f32[1024,256]{1,0:T(8,128)}) %reduce-scatter.20.cloned.1.call-update) | async-done | bytes 1048592 | tf_op jit(solution)/shard_map/reduce_scatter | solution.py:64
  314.6 6.0 all-reduce.9
  326.3 19.3 %all-gather.16.cloned.1.call-done = bf16[1024,1024]{1,0:T(8,128)(2,1)} async-done(((bf16[1024,256]{1,0:T(8,128)(2,1)}), bf16[1024,1024]{1,0:T(8,128)(2,1)}) %all-gather.16.cloned.1.call-update) | async-done | bytes 2097168 | tf_op jit(solution)/shard_map/all_gather | solution.py:61
  345.6 5.2 fusion.136
  350.8 39.8 %all-gather.20.cloned.1.call-done = bf16[1024,704]{0,1:T(8,128)(2,1)} async-done(((bf16[128,704]{0,1:T(8,128)(2,1)}), bf16[1024,704]{0,1:T(8,128)(2,1)}) %all-gather.20.cloned.1.call-update) | async-done | bytes 1441808 | tf_op jit(solution)/shard_map/all_gather | solution.py:54
  390.7 5.3 fusion.137
  395.9 38.2 %all-gather.22.cloned.1.call-done = bf16[704,1024]{1,0:T(8,128)(2,1)} async-done(((bf16[704,128]{1,0:T(8,128)(2,1)}), bf16[704,1024]{1,0:T(8,128)(2,1)}) %all-gather.22.cloned.1.call-update) | async-done | bytes 1441808 | tf_op jit(solution)/shard_map/all_gather | solution.py:55
  434.1 22.5 %all-gather.28.cloned.1.call-done = bf16[1024,1024]{1,0:T(8,128)(2,1)} async-done(((bf16[1024,256]{1,0:T(8,128)(2,1)}), bf16[1024,1024]{1,0:T(8,128)(2,1)}) %all-gather.28.cloned.1.call-update) | async-done | bytes 2097168 | tf_op jit(solution)/shard_map/all_gather | solution.py:61
  456.6 7.6 multiply_convert_fusion.6
  466.7 3.9 convolution_add_fusion.3
  470.7 44.5 %reduce-scatter.24.cloned.1.call-done = f32[1024,256]{1,0:T(8,128)} async-done(((f32[1024,1024]{1,0:T(8,128)}), f32[1024,256]{1,0:T(8,128)}) %reduce-scatter.24.cloned.1.call-update) | async-done | bytes 1048592 | tf_op jit(solution)/shard_map/reduce_scatter | solution.py:64
  515.1 3.0 multiply_reduce_fusion.5
  519.2 21.7 %all-gather.26.cloned.1.call-done = bf16[1024,1024]{1,0:T(8,128)(2,1)} async-done(((bf16[1024,256]{1,0:T(8,128)(2,1)}), bf16[1024,1024]{1,0:T(8,128)(2,1)}) %all-gather.26.cloned.1.call-update) | async-done | bytes 2097168 | tf_op jit(solution)/shard_map/all_gather | solution.py:61
  540.9 5.4 fusion.141
  546.3 3.2 fusion.140
  549.6 15.5 %all-gather.32.cloned.1.call-done = bf16[1024,1024]{1,0:T(8,128)(2,1)} async-done(((bf16[1024,256]{1,0:T(8,128)(2,1)}), bf16[1024,1024]{1,0:T(8,128)(2,1)}) %all-gather.32.cloned.1.call-update) | async-done | bytes 2097168 | tf_op jit(solution)/shard_map/all_gather | solution.py:61
  565.1 7.7 multiply_convert_fusion.4
  575.2 3.9 convolution_add_fusion.2
  579.2 44.6 %reduce-scatter.28.cloned.1.call-done = f32[1024,256]{1,0:T(8,128)} async-done(((f32[1024,1024]{1,0:T(8,128)}), f32[1024,256]{1,0:T(8,128)}) %reduce-scatter.28.cloned.1.call-update) | async-done | bytes 1048592 | tf_op jit(solution)/shard_map/reduce_scatter | solution.py:64
  625.5 5.9 all-reduce.8
  631.5 2.9 fusion.124
  635.3 22.9 %all-gather.30.cloned.1.call-done = bf16[1024,1024]{1,0:T(8,128)(2,1)} async-done(((bf16[1024,256]{1,0:T(8,128)(2,1)}), bf16[1024,1024]{1,0:T(8,128)(2,1)}) %all-gather.30.cloned.1.call-update) | async-done | bytes 2097168 | tf_op jit(solution)/shard_map/all_gather | solution.py:61
  663.8 63.1 %while.76 = (s32[]{:T(128)}, bf16[4,1024,64]{1,2,0:T(8,128)(2,1)}, bf16[4,1024,64]{1,2,0:T(8,128)(2,1)}, bf16[4,1024,64]{1,2,0:T(8,128)(2,1)}, s32[1024]{0:T(102...) while((s32[]{:T(128)}, bf16[4,1024,64]{1,2,0:T(8,128)(2,1)}, ...), condition=%wide.region_30.31_spmd.clone, body=%wide.region_27.30_spmd.clone.sunk | while | flops 512721408 | bytes 27057332 | solution.py:225
  726.9 3.4 convolution_convert_fusion
  734.2 2.8 add_add_fusion.1
  739.8 63.3 %while.77 = (s32[]{:T(128)}, bf16[4,1024,64]{1,2,0:T(8,128)(2,1)}, bf16[4,1024,64]{1,2,0:T(8,128)(2,1)}, bf16[4,1024,64]{1,2,0:T(8,128)(2,1)}, s32[1024]{0:T(102...) while((s32[]{:T(128)}, bf16[4,1024,64]{1,2,0:T(8,128)(2,1)}, ...), condition=%wide.region_40.41_spmd.clone, body=%wide.region_37.40_spmd.clone.sunk | while | flops 512721408 | bytes 27057332 | solution.py:225
  806.4 2.7 add_add_fusion
  810.5 5.3 fusion.138
  815.8 5.4 fusion.142
  822.8 3.2 fusion.155
  826.0 3.2 convolution_add_fusion.4
  829.6 3.2 fusion.154
  832.8 3.3 convolution_add_fusion.5
  837.7 3.2 fusion.153
  840.9 3.3 convolution_add_fusion.6
  845.2 2.4 fusion.152
  863.1 3.1 fusion.107
  866.6 21.1 %all-reduce.6 = (f32[1024]{0:T(1024)S(1)}, f32[1024]{0:T(1024)S(1)}) all-reduce(f32[1024]{0:T(1024)S(1)} %add_dynamic-update-slice_fusion.1, f32[1024]{0:T(1024)S(1)} %add_dynamic-update-slice_fusion), channel_id=26, replica_groups=mesh['row'=8,'col'=4] {'row'}, use_global_device_ids=true, to_apply=%region_60.61.clone | all-reduce | flops 2048 | bytes 16384
  887.9 7.3 all-reduce.7
  895.3 6.0 reduce-scatter.18.cloned.1.call-done
  901.2 3.4 fusion.105
  904.6 43.9 %reduce-scatter.22.cloned.1.call-done = f32[1024,256]{1,0:T(8,128)} async-done(((f32[1024,1024]{1,0:T(8,128)}), f32[1024,256]{1,0:T(8,128)}) %reduce-scatter.22.cloned.1.call-update) | async-done | bytes 1048592 | tf_op jit(solution)/shard_map/reduce_scatter | solution.py:64
  948.5 2.5 fusion.113
  954.1 70.7 %reduce-scatter.42.cloned.1.call-done = f32[128,704]{0,1:T(8,128)} async-done(((f32[1024,704]{0,1:T(8,128)}), f32[128,704]{0,1:T(8,128)}) %reduce-scatter.42.cloned.1.call-update) | async-done | bytes 360464 | tf_op jit(solution)/shard_map/reduce_scatter | solution.py:258
  1024.8 75.6 %reduce-scatter.40.cloned.1.call-done = f32[128,704]{0,1:T(8,128)} async-done(((f32[1024,704]{0,1:T(8,128)}), f32[128,704]{0,1:T(8,128)}) %reduce-scatter.40.cloned.1.call-update) | async-done | bytes 360464 | tf_op jit(solution)/shard_map/reduce_scatter | solution.py:257
  1100.4 75.4 %reduce-scatter.44.cloned.1.call-done = f32[704,128]{1,0:T(8,128)} async-done(((f32[704,1024]{1,0:T(8,128)}), f32[704,128]{1,0:T(8,128)}) %reduce-scatter.44.cloned.1.call-update) | async-done | bytes 360464 | tf_op jit(solution)/shard_map/reduce_scatter | solution.py:259
  1175.8 67.1 %reduce-scatter.38.cloned.1.call-done = f32[256,128]{1,0:T(8,128)} async-done(((f32[256,1024]{1,0:T(8,128)}), f32[256,128]{1,0:T(8,128)}) %reduce-scatter.38.cloned.1.call-update) | async-done | bytes 131088 | tf_op jit(solution)/shard_map/reduce_scatter | solution.py:256
  1242.9 66.7 %reduce-scatter.36.cloned.1.call-done = f32[128,256]{1,0:T(8,128)} async-done(((f32[1024,256]{1,0:T(8,128)}), f32[128,256]{1,0:T(8,128)}) %reduce-scatter.36.cloned.1.call-update) | async-done | bytes 131088 | tf_op jit(solution)/shard_map/reduce_scatter | solution.py:255
  1309.6 66.2 %reduce-scatter.34.cloned.1.call-done = f32[128,256]{1,0:T(8,128)} async-done(((f32[1024,256]{1,0:T(8,128)}), f32[128,256]{1,0:T(8,128)}) %reduce-scatter.34.cloned.1.call-update) | async-done | bytes 131088 | tf_op jit(solution)/shard_map/reduce_scatter | solution.py:254
  1375.8 66.7 %reduce-scatter.32.cloned.1.call-done = f32[128,256]{1,0:T(8,128)} async-done(((f32[1024,256]{1,0:T(8,128)}), f32[128,256]{1,0:T(8,128)}) %reduce-scatter.32.cloned.1.call-update) | async-done | bytes 131088 | tf_op jit(solution)/shard_map/reduce_scatter | solution.py:253
  (522 shorter events, 274.0 us)
Async XLA Ops:
  8.0 158.5 %all-gather.14.cloned.1.call-start = ((), (), s32[]{:S(2)}) async-start(), calls=%async_computation.15 | async-start | bytes 2621440 | tf_op jit(solution)/shard_map/all_gather | solution.py:61
  30.4 11.0 copy-start.36
  31.9 41.1 %copy-start.37 = (bf16[128,256]{1,0:T(8,128)(2,1)S(1)}, bf16[128,256]{1,0:T(8,128)(2,1)}, u32[]{:S(2)}) copy-start(bf16[128,256]{1,0:T(8,128)(2,1)} %param.46) | copy-start | bytes 196612
  32.1 9.2 copy-start.44
  37.8 3.5 copy-start.46
  37.8 3.5 copy-start.48
  37.8 3.5 copy-start.40
  37.9 3.5 copy-start.42
  37.9 66.6 %copy-start.38 = (bf16[128,256]{1,0:T(8,128)(2,1)S(1)}, bf16[128,256]{1,0:T(8,128)(2,1)}, u32[]{:S(2)}) copy-start(bf16[128,256]{1,0:T(8,128)(2,1)} %param.47) | copy-start | bytes 196612
  37.9 100.0 %copy-start.55 = (s32[2]{0:T(128)S(1)}, s32[2]{0:T(128)}, u32[]{:S(2)}) copy-start(s32[2]{0:T(128)} %param.54) | copy-start | bytes 28
  37.9 100.6 %copy-start.39 = (bf16[256,128]{1,0:T(8,128)(2,1)S(1)}, bf16[256,128]{1,0:T(8,128)(2,1)}, u32[]{:S(2)}) copy-start(bf16[256,128]{1,0:T(8,128)(2,1)} %param.48) | copy-start | bytes 196612
  40.5 177.6 %all-gather.24.cloned.1.call-start = ((), (), s32[]{:S(2)}) async-start(), calls=%async_computation.22 | async-start | bytes 2621440 | tf_op jit(solution)/shard_map/all_gather | solution.py:61
  41.2 245.8 %reduce-scatter.16.cloned.1.call-start = ((), (), s32[]{:S(2)}) async-start(), calls=%async_computation.16 | async-start | bytes 5242880 | tf_op jit(solution)/shard_map/reduce_scatter | solution.py:64
  73.0 96.8 %copy-start.13 = (bf16[1024,256]{1,0:T(8,128)(2,1)}, bf16[1024,256]{1,0:T(8,128)(2,1)S(1)}, u32[]{:S(2)}) copy-start(bf16[1024,256]{1,0:T(8,128)(2,1)S(1)} %all_gather.36) | copy-start | bytes 1572868
  104.5 67.7 %copy-start.17 = (bf16[1024,256]{1,0:T(8,128)(2,1)}, bf16[1024,256]{1,0:T(8,128)(2,1)S(1)}, u32[]{:S(2)}) copy-start(bf16[1024,256]{1,0:T(8,128)(2,1)S(1)} %all_gather.37) | copy-start | bytes 1572868
  166.5 5.7 copy-start
  172.2 4.0 copy-start.28
  217.8 6.7 copy-start.18
  217.8 94.9 %reduce-scatter.20.cloned.1.call-start = ((), (), s32[]{:S(2)}) async-start(), calls=%async_computation.23 | async-start | bytes 5242880 | tf_op jit(solution)/shard_map/reduce_scatter | solution.py:64
  218.8 5.7 copy-start.2
  224.4 3.9 copy-start.29
  270.0 42.7 %copy-start.6 = (bf16[2048,256]{1,0:T(8,128)(2,1)S(1)}, bf16[2048,256]{1,0:T(8,128)(2,1)}, u32[]{:S(2)}) copy-start(bf16[2048,256]{1,0:T(8,128)(2,1)} %param.44) | copy-start | bytes 3145732
  270.1 56.2 %all-gather.18.cloned.1.call-start = ((), (), s32[]{:S(2)}) async-start(), calls=%async_computation.18 | async-start | bytes 1622016 | tf_op jit(solution)/shard_map/all_gather | solution.py:53
  270.6 75.0 %all-gather.16.cloned.1.call-start = ((), (), s32[]{:S(2)}) async-start(), calls=%async_computation.17 | async-start | bytes 2621440 | tf_op jit(solution)/shard_map/all_gather | solution.py:61
  314.6 316.8 %copy-start.8 = (f32[1024,256]{1,0:T(8,128)}, f32[1024,256]{1,0:T(8,128)S(1)}, u32[]{:S(2)}) copy-start(f32[1024,256]{1,0:T(8,128)S(1)} %get-tuple-element.830) | copy-start | bytes 3145732
  314.6 9.8 copy-start.35
  321.7 69.0 %all-gather.20.cloned.1.call-start = ((), (), s32[]{:S(2)}) async-start(), calls=%async_computation.19 | async-start | bytes 1622016 | tf_op jit(solution)/shard_map/all_gather | solution.py:54
  322.2 111.9 %all-gather.22.cloned.1.call-start = ((), (), s32[]{:S(2)}) async-start(), calls=%async_computation.20 | async-start | bytes 1622016 | tf_op jit(solution)/shard_map/all_gather | solution.py:55
  323.0 133.6 %all-gather.28.cloned.1.call-start = ((), (), s32[]{:S(2)}) async-start(), calls=%async_computation.26 | async-start | bytes 2621440 | tf_op jit(solution)/shard_map/all_gather | solution.py:61
  324.3 26.5 %copy-start.50 = (pred[1024]{0:T(1024)(128)(4,1)}, pred[1024]{0:T(1024)(128)(4,1)S(1)}, u32[]{:S(2)}) copy-start(pred[1024]{0:T(1024)(128)(4,1)S(1)} %get-tuple-element.888) | copy-start | bytes 3076
  324.3 26.5 %copy-start.52 = (pred[1024]{0:T(1024)(128)(4,1)}, pred[1024]{0:T(1024)(128)(4,1)S(1)}, u32[]{:S(2)}) copy-start(pred[1024]{0:T(1024)(128)(4,1)S(1)} %get-tuple-element.889) | copy-start | bytes 3076
  325.9 189.2 %reduce-scatter.24.cloned.1.call-start = ((), (), s32[]{:S(2)}) async-start(), calls=%async_computation.27 | async-start | bytes 5242880 | tf_op jit(solution)/shard_map/reduce_scatter | solution.py:64
  456.6 7.6 copy-start.64
  470.6 70.3 %all-gather.26.cloned.1.call-start = ((), (), s32[]{:S(2)}) async-start(), calls=%async_computation.24 | async-start | bytes 2621440 | tf_op jit(solution)/shard_map/all_gather | solution.py:61
  518.1 47.0 %all-gather.32.cloned.1.call-start = ((), (), s32[]{:S(2)}) async-start(), calls=%async_computation.30 | async-start | bytes 2621440 | tf_op jit(solution)/shard_map/all_gather | solution.py:61
  518.7 105.1 %reduce-scatter.28.cloned.1.call-start = ((), (), s32[]{:S(2)}) async-start(), calls=%async_computation.31 | async-start | bytes 5242880 | tf_op jit(solution)/shard_map/reduce_scatter | solution.py:64
  540.9 5.4 copy-start.60
  540.9 5.4 copy-start.65
  565.1 7.7 copy-start.66
  579.1 79.2 %all-gather.30.cloned.1.call-start = ((), (), s32[]{:S(2)}) async-start(), calls=%async_computation.28 | async-start | bytes 2621440 | tf_op jit(solution)/shard_map/all_gather | solution.py:61
  623.8 7.6 copy-start.10
  634.4 92.5 %all-gather.34.cloned.1.call-start = ((), (), s32[]{:S(2)}) async-start(), calls=%async_computation.32 | async-start | bytes 2621440 | tf_op jit(solution)/shard_map/all_gather | solution.py:61
  635.1 227.9 %reduce-scatter.26.cloned.1.call-start = ((), (), s32[]{:S(2)}) async-start(), calls=%async_computation.29 | async-start | bytes 5242880 | tf_op jit(solution)/shard_map/reduce_scatter | solution.py:64
  726.9 4.9 copy-start.19
  726.9 4.9 copy-start.21
  737.0 126.1 %reduce-scatter.30.cloned.1.call-start = ((), (), s32[]{:S(2)}) async-start(), calls=%async_computation.33 | async-start | bytes 5242880 | tf_op jit(solution)/shard_map/reduce_scatter | solution.py:64
  809.2 92.0 %reduce-scatter.18.cloned.1.call-start = ((), (), s32[]{:S(2)}) async-start(), calls=%async_computation.21 | async-start | bytes 5242880 | tf_op jit(solution)/shard_map/reduce_scatter | solution.py:64
  815.8 132.7 %reduce-scatter.22.cloned.1.call-start = ((), (), s32[]{:S(2)}) async-start(), calls=%async_computation.25 | async-start | bytes 5242880 | tf_op jit(solution)/shard_map/reduce_scatter | solution.py:64
  821.2 203.6 %reduce-scatter.42.cloned.1.call-start = ((), (), s32[]{:S(2)}) async-start(), calls=%async_computation.39 | async-start | bytes 3244032 | tf_op jit(solution)/shard_map/reduce_scatter | solution.py:258
  822.8 3.2 copy-start.72
  829.2 271.2 %reduce-scatter.40.cloned.1.call-start = ((), (), s32[]{:S(2)}) async-start(), calls=%async_computation.38 | async-start | bytes 3244032 | tf_op jit(solution)/shard_map/reduce_scatter | solution.py:257
  829.5 3.2 copy-start.62
  829.6 3.2 copy-start.75
  836.0 339.7 %reduce-scatter.44.cloned.1.call-start = ((), (), s32[]{:S(2)}) async-start(), calls=%async_computation.40 | async-start | bytes 3244032 | tf_op jit(solution)/shard_map/reduce_scatter | solution.py:259
  844.2 398.7 %reduce-scatter.38.cloned.1.call-start = ((), (), s32[]{:S(2)}) async-start(), calls=%async_computation.37 | async-start | bytes 1179648 | tf_op jit(solution)/shard_map/reduce_scatter | solution.py:256
  849.4 460.2 %reduce-scatter.36.cloned.1.call-start = ((), (), s32[]{:S(2)}) async-start(), calls=%async_computation.36 | async-start | bytes 1179648 | tf_op jit(solution)/shard_map/reduce_scatter | solution.py:255
  853.3 522.6 %reduce-scatter.34.cloned.1.call-start = ((), (), s32[]{:S(2)}) async-start(), calls=%async_computation.35 | async-start | bytes 1179648 | tf_op jit(solution)/shard_map/reduce_scatter | solution.py:254
  857.2 585.4 %reduce-scatter.32.cloned.1.call-start = ((), (), s32[]{:S(2)}) async-start(), calls=%async_computation.34 | async-start | bytes 1179648 | tf_op jit(solution)/shard_map/reduce_scatter | solution.py:253
  863.0 32.2 %copy-start.49 = (f32[1024]{0:T(1024)S(1)}, f32[1024]{0:T(1024)}, u32[]{:S(2)}) copy-start(f32[1024]{0:T(1024)} %copy-done.48) | copy-start | bytes 12292
  863.0 32.2 %copy-start.47 = (f32[1024]{0:T(1024)S(1)}, f32[1024]{0:T(1024)}, u32[]{:S(2)}) copy-start(f32[1024]{0:T(1024)} %copy-done.46) | copy-start | bytes 12292
  863.0 38.2 %copy-start.9 = (f32[1024,256]{1,0:T(8,128)S(1)}, f32[1024,256]{1,0:T(8,128)}, u32[]{:S(2)}) copy-start(f32[1024,256]{1,0:T(8,128)} %copy-done.8) | copy-start | bytes 3145732
  863.0 38.2 %copy-start.53 = (pred[1024]{0:T(1024)(128)(4,1)S(1)}, pred[1024]{0:T(1024)(128)(4,1)}, u32[]{:S(2)}) copy-start(pred[1024]{0:T(1024)(128)(4,1)} %copy-done.52) | copy-start | bytes 3076
  895.2 53.2 %copy-start.51 = (pred[1024]{0:T(1024)(128)(4,1)S(1)}, pred[1024]{0:T(1024)(128)(4,1)}, u32[]{:S(2)}) copy-start(pred[1024]{0:T(1024)(128)(4,1)} %copy-done.50) | copy-start | bytes 3076
  904.6 46.4 %copy-start.34 = (bf16[1024,256]{1,0:T(8,128)(2,1)S(1)}, bf16[1024,256]{1,0:T(8,128)(2,1)}, u32[]{:S(2)}) copy-start(bf16[1024,256]{1,0:T(8,128)(2,1)} %get-tuple-element.874) | copy-start | bytes 1572868
  (39 other events, 72.8 us)
Sparse Core Ops, SparseCore 0:
  40.6 20.3 all-gather.13
  63.1 22.8 all-gather.23
  217.9 42.5 reduce-scatter.15
  270.2 42.4 reduce-scatter.19
  579.3 44.5 reduce-scatter.27
  737.1 44.5 reduce-scatter.25
  809.3 44.3 reduce-scatter.29
  856.3 44.9 reduce-scatter.17
  903.9 44.5 reduce-scatter.21
  952.5 72.3 reduce-scatter.41
  1029.0 71.4 reduce-scatter.39
  1104.4 71.3 reduce-scatter.43
  1179.7 63.1 reduce-scatter.37
  1247.1 62.4 reduce-scatter.35
  1313.5 62.3 reduce-scatter.33
  1380.0 62.4 reduce-scatter.31
Sparse Core Ops, SparseCore 1:
  272.6 41.1 all-gather.17
  321.7 23.8 all-gather.15
  347.5 43.1 all-gather.19
  392.7 41.3 all-gather.21
  435.7 20.9 all-gather.27
  470.7 44.4 reduce-scatter.23
  518.2 22.6 all-gather.25
  542.4 22.7 all-gather.31
  634.5 23.8 all-gather.29
  659.9 22.7 all-gather.33
where the time goes:
time: 1460 us; the launch traced here: 1450 us
  waiting for transfers between devices  837 us (57%)
  matrix products  278 us (19%)
  blocking collectives  209 us (14%)
  other arithmetic  71 us (5%)
  local copies, waits for them, and re-layouts  33.4 us (2%)
  between operations  17.7 us (1%)
    reduce_scatter x8, waiting for transfers between devices, reduce_cols(): lax.psum_scatter(partial_value, 'col', scatter_dimension=1, tiled=True)  165 us
    dot_general x62, matrix products, times_trans(): lax.dot_general(left, right, (((1,), (1,)), ((), ())), preferred_element_...  117 us
    all_gather x8, waiting for transfers between devices, to_full(): return lax.all_gather(values_own, 'col', axis=1, tiled=True)  102 us
    reduce_scatter x1, waiting for transfers between devices, shards(): lax.psum_scatter(local_terms[4], 'row', scatter_dimension=0, tiled=True)  75.6 us
    reduce_scatter x1, waiting for transfers between devices, shards(): lax.psum_scatter(local_terms[6], 'row', scatter_dimension=1, tiled=True)  75.4 us
    reduce_scatter x1, waiting for transfers between devices, shards(): lax.psum_scatter(local_terms[5], 'row', scatter_dimension=0, tiled=True)  70.7 us
    dot_general x46, matrix products, contract_rows(): lax.dot_general(left, right, (((0,), (0,)), ((), ())), preferred_element_...  69.9 us
    reduce_scatter x1, waiting for transfers between devices, shards(): lax.psum_scatter(local_terms[3], 'row', scatter_dimension=1, tiled=True)  67.1 us
  transfers between devices with their start and end apart: 26, of which 19 were waited for; matrix products, arithmetic and copies ran while one was open for 22% of the time, Pallas kernels for 0%

commit v1 on v0

--- a/solution.py
+++ b/solution.py
@@ -45,8 +45,28 @@
     positions = lax.iota(jnp.int32, seq)
 
     def fetch():
+
+        def _clear_view(dim_at, sheet):
+            mesh_ax = "row"
+            cores_n = lax.psum(1, mesh_ax)
+            steps_seen = [(q, (q + 1) % cores_n) for q in range(cores_n)]
+            copies = [(q, (q - 1) % cores_n) for q in range(cores_n)]
+            piece_next, a_now = ([sheet], [sheet])
+            for _ in range(cores_n // 2):
+                piece_next.append(lax.ppermute(piece_next[-1], mesh_ax, steps_seen))
+            w = 0
+            while w < (cores_n - 1) // 2:
+                a_now.append(lax.ppermute(a_now[-1], mesh_ax, copies))
+                w += 1
+            prior = jnp.roll(
+                jnp.concatenate([*piece_next[::-1], *a_now[1:]], dim_at),
+                (lax.axis_index(mesh_ax) - cores_n // 2) * sheet.shape[dim_at],
+                dim_at,
+            )
+            return prior
+
         return (
-            lax.all_gather(w_query, "row", axis=0, tiled=True),
+            _clear_view(0, w_query),
             lax.all_gather(w_key, "row", axis=0, tiled=True),
             lax.all_gather(w_value, "row", axis=0, tiled=True),
             lax.all_gather(w_out, "row", axis=1, tiled=True),

time: 1460 us -> 1450 us (level)
  blocking collectives: 209 us -> 182 us
    all_gather x1 -> x0, blocking collectives: 31.7 us -> none  [fetch(): lax.all_gather(w_query, 'row', axis=0, tiled=True)]
  transfers between devices with their start and end apart: 26 -> 33, of which waited for: 19 -> 21; matrix products, arithmetic and copies ran while one was open for 22% -> 23% of each run, Pallas kernels for 0% -> 0%
where the time goes in v1:
time: 1450 us; the launch traced here: 1440 us
  waiting for transfers between devices  839 us (58%)
  matrix products  278 us (19%)
  blocking collectives  182 us (13%)
  other arithmetic  73.2 us (5%)
  local copies, waits for them, and re-layouts  33.7 us (2%)
  between operations  17.7 us (1%)
  starting transfers between devices  14.8 us (1%)
    reduce_scatter x8, waiting for transfers between devices, reduce_cols(): lax.psum_scatter(partial_value, 'col', scatter_dimension=1, tiled=True)  163 us
    dot_general x62, matrix products, times_trans(): lax.dot_general(left, right, (((1,), (1,)), ((), ())), preferred_element_...  117 us
    all_gather x8, waiting for transfers between devices, to_full(): return lax.all_gather(values_own, 'col', axis=1, tiled=True)  102 us
    reduce_scatter x1, waiting for transfers between devices, shards(): lax.psum_scatter(local_terms[4], 'row', scatter_dimension=0, tiled=True)  75.8 us
    reduce_scatter x1, waiting for transfers between devices, shards(): lax.psum_scatter(local_terms[6], 'row', scatter_dimension=1, tiled=True)  75.5 us
    reduce_scatter x1, waiting for transfers between devices, shards(): lax.psum_scatter(local_terms[5], 'row', scatter_dimension=0, tiled=True)  70.6 us
    dot_general x46, matrix products, contract_rows(): lax.dot_general(left, right, (((0,), (0,)), ((), ())), preferred_element_...  69.9 us
    reduce_scatter x1, waiting for transfers between devices, shards(): lax.psum_scatter(local_terms[3], 'row', scatter_dimension=1, tiled=True)  67.1 us
  transfers between devices with their start and end apart: 33, of which 21 were waited for; matrix products, arithmetic and copies ran while one was open for 23% of the time, Pallas kernels for 0%

profile of v1, /device:TPU:0, one launch (start us, length us, event | category | flops | bytes accessed | tf_op | source)
XLA Modules:
  0.0 1439.0 jit_solution(17949099206993580704)
XLA Ops:
  8.1 22.3 %all-gather = bf16[8,1,128]{2,1,0:T(2,128)(2,1)S(1)} all-gather(bf16[1,1,128]{2,1,0:T(2,128)(2,1)} %bitcast.471), channel_id=1, replica_groups=mesh['row'=8,'col'=4] {'row'}, dimensions={0}, use_global_device_ids=true | all-gather | bytes 2304 | tf_op jit(solution)/shard_map/all_gather | solution.py:76
  32.1 5.7 all-reduce.10
  38.4 2.5 fusion.102
  41.1 4.7 collective-permute-start.4
  45.9 31.4 %all_gather.34 = bf16[1024,256]{1,0:T(8,128)(2,1)S(1)} all-gather(bf16[128,256]{1,0:T(8,128)(2,1)S(1)} %copy-done.35), channel_id=1, replica_groups=mesh['row'=8,'col'=4] {'row'}, dimensions={0}, use_global_device_ids=true | all-gather | bytes 589824 | tf_op jit(solution)/shard_map/all_gather | solution.py:70
  77.5 31.7 %all_gather.35 = bf16[1024,256]{1,0:T(8,128)(2,1)S(1)} all-gather(bf16[128,256]{1,0:T(8,128)(2,1)S(1)} %copy-done.36), channel_id=1, replica_groups=mesh['row'=8,'col'=4] {'row'}, dimensions={0}, use_global_device_ids=true | all-gather | bytes 589824 | tf_op jit(solution)/shard_map/all_gather | solution.py:71
  110.8 28.9 %all_gather.72 = bf16[256,1024]{1,0:T(8,128)(2,1)} all-gather(bf16[256,128]{1,0:T(8,128)(2,1)S(1)} %copy-done.37), channel_id=1, replica_groups=mesh['row'=8,'col'=4] {'row'}, dimensions={1}, use_global_device_ids=true | all-gather | bytes 589824 | tf_op jit(solution)/shard_map/all_gather | solution.py:72
  144.0 3.5 collective-permute-start.6
  151.7 3.4 convolution_convert_fusion.7
  164.3 34.7 %while.74 = (s32[]{:T(128)}, bf16[4,1024,64]{1,2,0:T(8,128)(2,1)}, f32[4,1024]{1,0:T(4,128)S(1)}, s32[1024]{0:T(1024)S(1)}, s32[]{:T(128)}, /*index=5*/bf16[4,10...) while((s32[]{:T(128)}, bf16[4,1024,64]{1,2,0:T(8,128)(2,1)}, ...), condition=%wide.region_7.9_spmd.clone, body=%wide.region_2.8_spmd.clone.sunk | while | flops 209454592 | bytes 10959497 | solution.py:169
  199.0 3.9 fusion.136
  203.9 3.3 convolution_convert_fusion.4
  216.5 34.8 %while.75 = (s32[]{:T(128)}, bf16[4,1024,64]{1,2,0:T(8,128)(2,1)}, f32[4,1024]{1,0:T(4,128)S(1)}, s32[1024]{0:T(1024)S(1)}, s32[]{:T(128)}, /*index=5*/bf16[4,10...) while((s32[]{:T(128)}, bf16[4,1024,64]{1,2,0:T(8,128)(2,1)}, ...), condition=%wide.region_19.21_spmd.clone, body=%wide.region_14.20_spmd.clone.sunk | while | flops 209454592 | bytes 10959497 | solution.py:169
  251.2 4.0 fusion.140
  255.9 21.3 %all-gather.1 = bf16[8,1,128]{2,1,0:T(2,128)(2,1)S(1)} all-gather(bf16[1,1,128]{2,1,0:T(2,128)(2,1)S(1)} %bitcast.472), channel_id=1, replica_groups=mesh['row'=8,'col'=4] {'row'}, dimensions={0}, use_global_device_ids=true | all-gather | bytes 2304 | tf_op jit(solution)/shard_map/all_gather | solution.py:77
  277.3 24.5 %reduce-scatter.20.cloned.1.call-done = f32[1024,256]{1,0:T(8,128)} async-done(((f32[1024,1024]{1,0:T(8,128)}), f32[1024,256]{1,0:T(8,128)}) %reduce-scatter.20.cloned.1.call-update) | async-done | bytes 1048592 | tf_op jit(solution)/shard_map/reduce_scatter | solution.py:84
  303.8 6.0 all-reduce.9
  315.4 19.4 %all-gather.16.cloned.1.call-done = bf16[1024,1024]{1,0:T(8,128)(2,1)} async-done(((bf16[1024,256]{1,0:T(8,128)(2,1)}), bf16[1024,1024]{1,0:T(8,128)(2,1)}) %all-gather.16.cloned.1.call-update) | async-done | bytes 2097168 | tf_op jit(solution)/shard_map/all_gather | solution.py:81
  334.8 5.2 fusion.137
  340.0 39.8 %all-gather.20.cloned.1.call-done = bf16[1024,704]{0,1:T(8,128)(2,1)} async-done(((bf16[128,704]{0,1:T(8,128)(2,1)}), bf16[1024,704]{0,1:T(8,128)(2,1)}) %all-gather.20.cloned.1.call-update) | async-done | bytes 1441808 | tf_op jit(solution)/shard_map/all_gather | solution.py:74
  379.8 5.3 fusion.138
  385.1 38.1 %all-gather.22.cloned.1.call-done = bf16[704,1024]{1,0:T(8,128)(2,1)} async-done(((bf16[704,128]{1,0:T(8,128)(2,1)}), bf16[704,1024]{1,0:T(8,128)(2,1)}) %all-gather.22.cloned.1.call-update) | async-done | bytes 1441808 | tf_op jit(solution)/shard_map/all_gather | solution.py:75
  423.3 22.5 %all-gather.28.cloned.1.call-done = bf16[1024,1024]{1,0:T(8,128)(2,1)} async-done(((bf16[1024,256]{1,0:T(8,128)(2,1)}), bf16[1024,1024]{1,0:T(8,128)(2,1)}) %all-gather.28.cloned.1.call-update) | async-done | bytes 2097168 | tf_op jit(solution)/shard_map/all_gather | solution.py:81
  445.8 7.6 multiply_convert_fusion.6
  455.8 3.9 convolution_add_fusion.3
  459.8 44.5 %reduce-scatter.24.cloned.1.call-done = f32[1024,256]{1,0:T(8,128)} async-done(((f32[1024,1024]{1,0:T(8,128)}), f32[1024,256]{1,0:T(8,128)}) %reduce-scatter.24.cloned.1.call-update) | async-done | bytes 1048592 | tf_op jit(solution)/shard_map/reduce_scatter | solution.py:84
  504.3 3.0 multiply_reduce_fusion.5
  508.1 21.9 %all-gather.26.cloned.1.call-done = bf16[1024,1024]{1,0:T(8,128)(2,1)} async-done(((bf16[1024,256]{1,0:T(8,128)(2,1)}), bf16[1024,1024]{1,0:T(8,128)(2,1)}) %all-gather.26.cloned.1.call-update) | async-done | bytes 2097168 | tf_op jit(solution)/shard_map/all_gather | solution.py:81
  530.1 5.4 fusion.142
  535.5 3.2 fusion.141
  538.8 15.5 %all-gather.32.cloned.1.call-done = bf16[1024,1024]{1,0:T(8,128)(2,1)} async-done(((bf16[1024,256]{1,0:T(8,128)(2,1)}), bf16[1024,1024]{1,0:T(8,128)(2,1)}) %all-gather.32.cloned.1.call-update) | async-done | bytes 2097168 | tf_op jit(solution)/shard_map/all_gather | solution.py:81
  554.3 7.6 multiply_convert_fusion.4
  564.4 3.9 convolution_add_fusion.2
  568.4 44.6 %reduce-scatter.28.cloned.1.call-done = f32[1024,256]{1,0:T(8,128)} async-done(((f32[1024,1024]{1,0:T(8,128)}), f32[1024,256]{1,0:T(8,128)}) %reduce-scatter.28.cloned.1.call-update) | async-done | bytes 1048592 | tf_op jit(solution)/shard_map/reduce_scatter | solution.py:84
  614.7 5.9 all-reduce.8
  620.6 2.9 fusion.125
  624.7 22.7 %all-gather.30.cloned.1.call-done = bf16[1024,1024]{1,0:T(8,128)(2,1)} async-done(((bf16[1024,256]{1,0:T(8,128)(2,1)}), bf16[1024,1024]{1,0:T(8,128)(2,1)}) %all-gather.30.cloned.1.call-update) | async-done | bytes 2097168 | tf_op jit(solution)/shard_map/all_gather | solution.py:81
  653.0 63.0 %while.76 = (s32[]{:T(128)}, bf16[4,1024,64]{1,2,0:T(8,128)(2,1)}, bf16[4,1024,64]{1,2,0:T(8,128)(2,1)}, bf16[4,1024,64]{1,2,0:T(8,128)(2,1)}, s32[1024]{0:T(102...) while((s32[]{:T(128)}, bf16[4,1024,64]{1,2,0:T(8,128)(2,1)}, ...), condition=%wide.region_30.32_spmd.clone, body=%wide.region_27.31_spmd.clone.sunk | while | flops 512721408 | bytes 27057332 | solution.py:245
  716.0 3.3 convolution_convert_fusion
  723.3 2.8 add_add_fusion.1
  728.9 63.3 %while.77 = (s32[]{:T(128)}, bf16[4,1024,64]{1,2,0:T(8,128)(2,1)}, bf16[4,1024,64]{1,2,0:T(8,128)(2,1)}, bf16[4,1024,64]{1,2,0:T(8,128)(2,1)}, s32[1024]{0:T(102...) while((s32[]{:T(128)}, bf16[4,1024,64]{1,2,0:T(8,128)(2,1)}, ...), condition=%wide.region_40.42_spmd.clone, body=%wide.region_37.41_spmd.clone.sunk | while | flops 512721408 | bytes 27057332 | solution.py:245
  795.5 2.7 add_add_fusion
  799.6 5.3 fusion.139
  804.9 5.4 fusion.143
  812.0 3.2 fusion.156
  815.2 3.2 convolution_add_fusion.4
  818.7 3.2 fusion.155
  821.9 3.3 convolution_add_fusion.5
  826.9 3.2 fusion.154
  830.0 3.3 convolution_add_fusion.6
  852.2 3.1 fusion.107
  855.8 20.9 %all-reduce.6 = (f32[1024]{0:T(1024)S(1)}, f32[1024]{0:T(1024)S(1)}) all-reduce(f32[1024]{0:T(1024)S(1)} %add_dynamic-update-slice_fusion.1, f32[1024]{0:T(1024)S(1)} %add_dynamic-update-slice_fusion), channel_id=26, replica_groups=mesh['row'=8,'col'=4] {'row'}, use_global_device_ids=true, to_apply=%region_60.62.clone | all-reduce | flops 2048 | bytes 16384
  876.9 7.3 all-reduce.7
  884.3 6.0 reduce-scatter.18.cloned.1.call-done
  890.2 3.4 fusion.105
  893.6 43.9 %reduce-scatter.22.cloned.1.call-done = f32[1024,256]{1,0:T(8,128)} async-done(((f32[1024,1024]{1,0:T(8,128)}), f32[1024,256]{1,0:T(8,128)}) %reduce-scatter.22.cloned.1.call-update) | async-done | bytes 1048592 | tf_op jit(solution)/shard_map/reduce_scatter | solution.py:84
  937.5 2.5 fusion.113
  943.1 70.6 %reduce-scatter.42.cloned.1.call-done = f32[128,704]{0,1:T(8,128)} async-done(((f32[1024,704]{0,1:T(8,128)}), f32[128,704]{0,1:T(8,128)}) %reduce-scatter.42.cloned.1.call-update) | async-done | bytes 360464 | tf_op jit(solution)/shard_map/reduce_scatter | solution.py:278
  1013.6 75.8 %reduce-scatter.40.cloned.1.call-done = f32[128,704]{0,1:T(8,128)} async-done(((f32[1024,704]{0,1:T(8,128)}), f32[128,704]{0,1:T(8,128)}) %reduce-scatter.40.cloned.1.call-update) | async-done | bytes 360464 | tf_op jit(solution)/shard_map/reduce_scatter | solution.py:277
  1089.4 75.5 %reduce-scatter.44.cloned.1.call-done = f32[704,128]{1,0:T(8,128)} async-done(((f32[704,1024]{1,0:T(8,128)}), f32[704,128]{1,0:T(8,128)}) %reduce-scatter.44.cloned.1.call-update) | async-done | bytes 360464 | tf_op jit(solution)/shard_map/reduce_scatter | solution.py:279
  1164.9 67.1 %reduce-scatter.38.cloned.1.call-done = f32[256,128]{1,0:T(8,128)} async-done(((f32[256,1024]{1,0:T(8,128)}), f32[256,128]{1,0:T(8,128)}) %reduce-scatter.38.cloned.1.call-update) | async-done | bytes 131088 | tf_op jit(solution)/shard_map/reduce_scatter | solution.py:276
  1232.0 66.6 %reduce-scatter.36.cloned.1.call-done = f32[128,256]{1,0:T(8,128)} async-done(((f32[1024,256]{1,0:T(8,128)}), f32[128,256]{1,0:T(8,128)}) %reduce-scatter.36.cloned.1.call-update) | async-done | bytes 131088 | tf_op jit(solution)/shard_map/reduce_scatter | solution.py:275
  1298.6 66.2 %reduce-scatter.34.cloned.1.call-done = f32[128,256]{1,0:T(8,128)} async-done(((f32[1024,256]{1,0:T(8,128)}), f32[128,256]{1,0:T(8,128)}) %reduce-scatter.34.cloned.1.call-update) | async-done | bytes 131088 | tf_op jit(solution)/shard_map/reduce_scatter | solution.py:274
  1364.9 66.6 %reduce-scatter.32.cloned.1.call-done = f32[128,256]{1,0:T(8,128)} async-done(((f32[1024,256]{1,0:T(8,128)}), f32[128,256]{1,0:T(8,128)}) %reduce-scatter.32.cloned.1.call-update) | async-done | bytes 131088 | tf_op jit(solution)/shard_map/reduce_scatter | solution.py:273
  (542 shorter events, 285.6 us)
Async XLA Ops:
  8.0 33.0 %copy-start.38 = (bf16[128,256]{1,0:T(8,128)(2,1)S(1)}, bf16[128,256]{1,0:T(8,128)(2,1)}, u32[]{:S(2)}) copy-start(bf16[128,256]{1,0:T(8,128)(2,1)} %param.47) | copy-start | bytes 196612
  8.0 143.6 %all-gather.14.cloned.1.call-start = ((), (), s32[]{:S(2)}) async-start(), calls=%async_computation.15 | async-start | bytes 2621440 | tf_op jit(solution)/shard_map/all_gather | solution.py:81
  30.4 15.5 %copy-start.35 = (bf16[128,256]{1,0:T(8,128)(2,1)S(1)}, bf16[128,256]{1,0:T(8,128)(2,1)}, u32[]{:S(2)}) copy-start(bf16[128,256]{1,0:T(8,128)(2,1)} %param.48) | copy-start | bytes 196612
  32.0 45.5 %copy-start.36 = (bf16[128,256]{1,0:T(8,128)(2,1)S(1)}, bf16[128,256]{1,0:T(8,128)(2,1)}, u32[]{:S(2)}) copy-start(bf16[128,256]{1,0:T(8,128)(2,1)} %param.49) | copy-start | bytes 196612
  32.1 45.3 %copy-start.43 = (f32[256]{0:T(256)}, f32[256]{0:T(256)S(1)}, u32[]{:S(2)}) copy-start(f32[256]{0:T(256)S(1)} %dynamic-slice_convert_fusion.1) | copy-start | bytes 3076
  37.9 39.5 %copy-start.39 = (f32[1024]{0:T(1024)}, f32[1024]{0:T(1024)S(1)}, u32[]{:S(2)}) copy-start(f32[1024]{0:T(1024)S(1)} %get-tuple-element.887) | copy-start | bytes 12292
  37.9 39.5 %copy-start.41 = (f32[1024]{0:T(1024)}, f32[1024]{0:T(1024)S(1)}, u32[]{:S(2)}) copy-start(f32[1024]{0:T(1024)S(1)} %get-tuple-element.888) | copy-start | bytes 12292
  38.4 72.4 %copy-start.37 = (bf16[256,128]{1,0:T(8,128)(2,1)S(1)}, bf16[256,128]{1,0:T(8,128)(2,1)}, u32[]{:S(2)}) copy-start(bf16[256,128]{1,0:T(8,128)(2,1)} %param.50) | copy-start | bytes 196612
  38.4 103.4 %copy-start.54 = (s32[2]{0:T(128)S(1)}, s32[2]{0:T(128)}, u32[]{:S(2)}) copy-start(s32[2]{0:T(128)} %param.56) | copy-start | bytes 28
  41.0 162.5 %all-gather.24.cloned.1.call-start = ((), (), s32[]{:S(2)}) async-start(), calls=%async_computation.22 | async-start | bytes 2621440 | tf_op jit(solution)/shard_map/all_gather | solution.py:81
  41.0 36.3 %collective-permute-start = (bf16[128,256]{1,0:T(8,128)(2,1)S(1)}, bf16[128,256]{1,0:T(8,128)(2,1)S(1)}, u32[]{:S(2)}, u32[]{:S(2)}) collective-permute-start(bf16[128,256]{1,0:T(8,128)(2,1)S(1)} %copy-done.38), channel_id=1, source_target_pairs={{0,4},{4,8},{8,12},{12,16},{16,20},{20,24},{24,28},{28,0},{1,5},{5... | collective-permute-start | bytes 196616 | tf_op jit(solution)/shard_map/ppermute | solution.py:56
  41.1 98.6 %collective-permute-start.4 = (bf16[128,256]{1,0:T(8,128)(2,1)S(1)}, bf16[128,256]{1,0:T(8,128)(2,1)S(1)}, u32[]{:S(2)}, u32[]{:S(2)}) collective-permute-start(bf16[128,256]{1,0:T(8,128)(2,1)S(1)} %copy-done.38), channel_id=1, source_target_pairs={{0,28},{4,0},{8,4},{12,8},{16,12},{20,16},{24,20},{28,24},{1,29},{... | collective-permute-start | bytes 196616 | tf_op jit(solution)/shard_map/ppermute | solution.py:59
  45.8 231.5 %reduce-scatter.16.cloned.1.call-start = ((), (), s32[]{:S(2)}) async-start(), calls=%async_computation.16 | async-start | bytes 5242880 | tf_op jit(solution)/shard_map/reduce_scatter | solution.py:84
  77.3 80.0 %copy-start.13 = (bf16[1024,256]{1,0:T(8,128)(2,1)}, bf16[1024,256]{1,0:T(8,128)(2,1)S(1)}, u32[]{:S(2)}) copy-start(bf16[1024,256]{1,0:T(8,128)(2,1)S(1)} %all_gather.34) | copy-start | bytes 1572868
  77.4 31.8 %collective-permute-start.1 = (bf16[128,256]{1,0:T(8,128)(2,1)S(1)}, bf16[128,256]{1,0:T(8,128)(2,1)S(1)}, u32[]{:S(2)}, u32[]{:S(2)}) collective-permute-start(bf16[128,256]{1,0:T(8,128)(2,1)S(1)} %collective-permute-done), channel_id=1, source_target_pairs={{0,4},{4,8},{8,12},{12,16},{16,20},{20,24},{24,28},{28,0},{1,5},{5... | collective-permute-start | bytes 196616 | tf_op jit(solution)/shard_map/ppermute | solution.py:56
  109.2 52.2 %copy-start.16 = (bf16[1024,256]{1,0:T(8,128)(2,1)}, bf16[1024,256]{1,0:T(8,128)(2,1)S(1)}, u32[]{:S(2)}) copy-start(bf16[1024,256]{1,0:T(8,128)(2,1)S(1)} %all_gather.35) | copy-start | bytes 1572868
  109.2 31.4 %collective-permute-start.2 = (bf16[128,256]{1,0:T(8,128)(2,1)S(1)}, bf16[128,256]{1,0:T(8,128)(2,1)S(1)}, u32[]{:S(2)}, u32[]{:S(2)}) collective-permute-start(bf16[128,256]{1,0:T(8,128)(2,1)S(1)} %collective-permute-done.1), channel_id=1, source_target_pairs={{0,4},{4,8},{8,12},{12,16},{16,20},{20,24},{24,28},{28,0},{1,5},{5... | collective-permute-start | bytes 196616 | tf_op jit(solution)/shard_map/ppermute | solution.py:56
  139.7 4.3 collective-permute-start.5
  140.6 7.0 collective-permute-start.3
  144.0 5.4 collective-permute-start.6
  151.7 5.7 copy-start
  202.9 6.7 copy-start.14
  202.9 98.9 %reduce-scatter.20.cloned.1.call-start = ((), (), s32[]{:S(2)}) async-start(), calls=%async_computation.23 | async-start | bytes 5242880 | tf_op jit(solution)/shard_map/reduce_scatter | solution.py:84
  203.9 5.7 copy-start.2
  255.2 46.7 %copy-start.6 = (bf16[2048,256]{1,0:T(8,128)(2,1)S(1)}, bf16[2048,256]{1,0:T(8,128)(2,1)}, u32[]{:S(2)}) copy-start(bf16[2048,256]{1,0:T(8,128)(2,1)} %param.46) | copy-start | bytes 3145732
  255.2 60.1 %all-gather.18.cloned.1.call-start = ((), (), s32[]{:S(2)}) async-start(), calls=%async_computation.18 | async-start | bytes 1622016 | tf_op jit(solution)/shard_map/all_gather | solution.py:73
  255.8 79.0 %all-gather.16.cloned.1.call-start = ((), (), s32[]{:S(2)}) async-start(), calls=%async_computation.17 | async-start | bytes 2621440 | tf_op jit(solution)/shard_map/all_gather | solution.py:81
  303.8 316.8 %copy-start.8 = (f32[1024,256]{1,0:T(8,128)}, f32[1024,256]{1,0:T(8,128)S(1)}, u32[]{:S(2)}) copy-start(f32[1024,256]{1,0:T(8,128)S(1)} %get-tuple-element.831) | copy-start | bytes 3145732
  303.8 9.8 copy-start.34
  310.8 69.0 %all-gather.20.cloned.1.call-start = ((), (), s32[]{:S(2)}) async-start(), calls=%async_computation.19 | async-start | bytes 1622016 | tf_op jit(solution)/shard_map/all_gather | solution.py:74
  311.4 111.8 %all-gather.22.cloned.1.call-start = ((), (), s32[]{:S(2)}) async-start(), calls=%async_computation.20 | async-start | bytes 1622016 | tf_op jit(solution)/shard_map/all_gather | solution.py:75
  312.1 133.6 %all-gather.28.cloned.1.call-start = ((), (), s32[]{:S(2)}) async-start(), calls=%async_computation.26 | async-start | bytes 2621440 | tf_op jit(solution)/shard_map/all_gather | solution.py:81
  313.5 26.5 %copy-start.49 = (pred[1024]{0:T(1024)(128)(4,1)}, pred[1024]{0:T(1024)(128)(4,1)S(1)}, u32[]{:S(2)}) copy-start(pred[1024]{0:T(1024)(128)(4,1)S(1)} %get-tuple-element.889) | copy-start | bytes 3076
  313.5 26.5 %copy-start.51 = (pred[1024]{0:T(1024)(128)(4,1)}, pred[1024]{0:T(1024)(128)(4,1)S(1)}, u32[]{:S(2)}) copy-start(pred[1024]{0:T(1024)(128)(4,1)S(1)} %get-tuple-element.890) | copy-start | bytes 3076
  315.1 189.2 %reduce-scatter.24.cloned.1.call-start = ((), (), s32[]{:S(2)}) async-start(), calls=%async_computation.27 | async-start | bytes 5242880 | tf_op jit(solution)/shard_map/reduce_scatter | solution.py:84
  445.8 7.6 copy-start.63
  459.8 70.3 %all-gather.26.cloned.1.call-start = ((), (), s32[]{:S(2)}) async-start(), calls=%async_computation.24 | async-start | bytes 2621440 | tf_op jit(solution)/shard_map/all_gather | solution.py:81
  507.3 47.0 %all-gather.32.cloned.1.call-start = ((), (), s32[]{:S(2)}) async-start(), calls=%async_computation.30 | async-start | bytes 2621440 | tf_op jit(solution)/shard_map/all_gather | solution.py:81
  507.9 105.1 %reduce-scatter.28.cloned.1.call-start = ((), (), s32[]{:S(2)}) async-start(), calls=%async_computation.31 | async-start | bytes 5242880 | tf_op jit(solution)/shard_map/reduce_scatter | solution.py:84
  530.1 5.4 copy-start.59
  530.1 5.4 copy-start.64
  554.3 7.7 copy-start.65
  568.3 79.1 %all-gather.30.cloned.1.call-start = ((), (), s32[]{:S(2)}) async-start(), calls=%async_computation.28 | async-start | bytes 2621440 | tf_op jit(solution)/shard_map/all_gather | solution.py:81
  613.0 7.6 copy-start.10
  623.5 92.5 %all-gather.34.cloned.1.call-start = ((), (), s32[]{:S(2)}) async-start(), calls=%async_computation.32 | async-start | bytes 2621440 | tf_op jit(solution)/shard_map/all_gather | solution.py:81
  624.3 227.9 %reduce-scatter.26.cloned.1.call-start = ((), (), s32[]{:S(2)}) async-start(), calls=%async_computation.29 | async-start | bytes 5242880 | tf_op jit(solution)/shard_map/reduce_scatter | solution.py:84
  716.0 4.9 copy-start.15
  716.0 4.9 copy-start.20
  726.1 126.1 %reduce-scatter.30.cloned.1.call-start = ((), (), s32[]{:S(2)}) async-start(), calls=%async_computation.33 | async-start | bytes 5242880 | tf_op jit(solution)/shard_map/reduce_scatter | solution.py:84
  798.3 92.0 %reduce-scatter.18.cloned.1.call-start = ((), (), s32[]{:S(2)}) async-start(), calls=%async_computation.21 | async-start | bytes 5242880 | tf_op jit(solution)/shard_map/reduce_scatter | solution.py:84
  804.9 132.6 %reduce-scatter.22.cloned.1.call-start = ((), (), s32[]{:S(2)}) async-start(), calls=%async_computation.25 | async-start | bytes 5242880 | tf_op jit(solution)/shard_map/reduce_scatter | solution.py:84
  810.4 203.2 %reduce-scatter.42.cloned.1.call-start = ((), (), s32[]{:S(2)}) async-start(), calls=%async_computation.39 | async-start | bytes 3244032 | tf_op jit(solution)/shard_map/reduce_scatter | solution.py:278
  818.4 271.0 %reduce-scatter.40.cloned.1.call-start = ((), (), s32[]{:S(2)}) async-start(), calls=%async_computation.38 | async-start | bytes 3244032 | tf_op jit(solution)/shard_map/reduce_scatter | solution.py:277
  825.2 339.7 %reduce-scatter.44.cloned.1.call-start = ((), (), s32[]{:S(2)}) async-start(), calls=%async_computation.40 | async-start | bytes 3244032 | tf_op jit(solution)/shard_map/reduce_scatter | solution.py:279
  833.4 398.6 %reduce-scatter.38.cloned.1.call-start = ((), (), s32[]{:S(2)}) async-start(), calls=%async_computation.37 | async-start | bytes 1179648 | tf_op jit(solution)/shard_map/reduce_scatter | solution.py:276
  838.6 460.1 %reduce-scatter.36.cloned.1.call-start = ((), (), s32[]{:S(2)}) async-start(), calls=%async_computation.36 | async-start | bytes 1179648 | tf_op jit(solution)/shard_map/reduce_scatter | solution.py:275
  842.4 522.4 %reduce-scatter.34.cloned.1.call-start = ((), (), s32[]{:S(2)}) async-start(), calls=%async_computation.35 | async-start | bytes 1179648 | tf_op jit(solution)/shard_map/reduce_scatter | solution.py:274
  846.4 585.1 %reduce-scatter.32.cloned.1.call-start = ((), (), s32[]{:S(2)}) async-start(), calls=%async_computation.34 | async-start | bytes 1179648 | tf_op jit(solution)/shard_map/reduce_scatter | solution.py:273
  852.1 32.1 %copy-start.48 = (f32[1024]{0:T(1024)S(1)}, f32[1024]{0:T(1024)}, u32[]{:S(2)}) copy-start(f32[1024]{0:T(1024)} %copy-done.47) | copy-start | bytes 12292
  852.1 32.1 %copy-start.46 = (f32[1024]{0:T(1024)S(1)}, f32[1024]{0:T(1024)}, u32[]{:S(2)}) copy-start(f32[1024]{0:T(1024)} %copy-done.45) | copy-start | bytes 12292
  852.1 38.1 %copy-start.9 = (f32[1024,256]{1,0:T(8,128)S(1)}, f32[1024,256]{1,0:T(8,128)}, u32[]{:S(2)}) copy-start(f32[1024,256]{1,0:T(8,128)} %copy-done.8) | copy-start | bytes 3145732
  852.1 38.1 %copy-start.52 = (pred[1024]{0:T(1024)(128)(4,1)S(1)}, pred[1024]{0:T(1024)(128)(4,1)}, u32[]{:S(2)}) copy-start(pred[1024]{0:T(1024)(128)(4,1)} %copy-done.51) | copy-start | bytes 3076
  884.3 53.2 %copy-start.50 = (pred[1024]{0:T(1024)(128)(4,1)S(1)}, pred[1024]{0:T(1024)(128)(4,1)}, u32[]{:S(2)}) copy-start(pred[1024]{0:T(1024)(128)(4,1)} %copy-done.49) | copy-start | bytes 3076
  893.6 46.4 %copy-start.33 = (bf16[1024,256]{1,0:T(8,128)(2,1)S(1)}, bf16[1024,256]{1,0:T(8,128)(2,1)}, u32[]{:S(2)}) copy-start(bf16[1024,256]{1,0:T(8,128)(2,1)} %get-tuple-element.875) | copy-start | bytes 1572868
  (45 other events, 87.5 us)
Sparse Core Ops, SparseCore 0:
  41.1 20.3 all-gather.13
  63.6 22.8 all-gather.23
  203.0 46.4 reduce-scatter.15
  255.3 46.4 reduce-scatter.19
  568.4 44.5 reduce-scatter.27
  726.3 44.5 reduce-scatter.25
  798.4 44.3 reduce-scatter.29
  845.3 44.8 reduce-scatter.17
  892.9 44.5 reduce-scatter.21
  941.4 72.1 reduce-scatter.41
  1017.8 71.5 reduce-scatter.39
  1093.4 71.4 reduce-scatter.43
  1168.9 63.0 reduce-scatter.37
  1236.2 62.3 reduce-scatter.35
  1302.5 62.3 reduce-scatter.33
  1369.1 62.3 reduce-scatter.31
Sparse Core Ops, SparseCore 1:
  257.7 45.1 all-gather.17
  310.9 23.8 all-gather.15
  336.7 43.1 all-gather.19
  381.9 41.3 all-gather.21
  424.8 20.9 all-gather.27
  459.8 44.4 reduce-scatter.23
  507.4 22.7 all-gather.25
  531.6 22.7 all-gather.31
  623.6 23.8 all-gather.29
  649.1 22.7 all-gather.33
